TPU v7x, 512 devices: a whole 4x4x16 slice. The times are simulated.
512 devices in a mesh: slab: 64 (over z_lo, x, core), grp: 8 (over z_hi, y).
Axes of the slice: x: 4, y: 4, z: 16 (z_hi: 2, z_lo: 8; z = z_hi * 8 + z_lo), core: 2. Of those that a mesh axis runs over, the one named last changes fastest.
Arguments:
- adj_out: float32 [5, 512, 256, 256], P(None, 'grp', 'slab'), may hold values from -6 to 6
- advect: bfloat16 [3, 512, 256, 256], P(None, 'grp', 'slab'), may hold values from -4 to 4
- viscosity: bfloat16 [512, 256, 256], P('grp', 'slab'), may hold values from 0.099609375 to 0.796875
- body_mask: int32 [512, 256, 256], P('grp', 'slab'), may hold values 0 or 1
- marker_x: int32 [2048], replicated, may hold values from 128 to 191
- marker_z: int32 [2048], replicated, may hold values from 0 to 255
- marker_y: int32 [2048], replicated, may hold values from 64 to 191
- drag_weight: float32 [2048], replicated, may hold values from -5 to 5
- inv_x: float32 [512, 512], P(None, 'grp'), may hold values from 0 to 1, as said below
- inv_y: float32 [256, 256], replicated, may hold values from 0 to 1, as said below
- inv_z: float32 [256, 256], replicated, may hold values from 0 to 1, as said below
Outputs:
- state_adjoint: float32 [5, 512, 256, 256], P(None, 'grp', 'slab')
Inputs may be any that keep to these rules, and one draw needn't show every extreme that they name: `inv_x`: entries of a given inverse. `inv_y`: entries of a given inverse. `inv_z`: entries of a given inverse.
All inputs are finite; a program needn't handle non-finite values. No bound on the sum of `body_mask` on one device may be relied on, other than what follows from the above.
Results may differ from a plain program's by a relative error of at most 0.0003.
Values sent between devices are 32-bit elements; how exact they have to be, the bound alone decides.
No kernel may reach another device: no remote copies, remote signals or barrier semaphores. Data moves between devices by JAX's collectives and lax.ppermute only.
A program may use at most 64 MiB of HBM per device.

v0:
```python
import jax
import jax.numpy as jnp
from jax import lax
from jax.sharding import PartitionSpec as P

time_step = 0.08
highest = lax.Precision.HIGHEST


def extended(cells, sides, width):
    for axis, dim in sides:
        count = lax.axis_size(axis)
        ends = count - 1
        head = lax.slice_in_dim(cells, 0, width, axis=dim)
        tail = lax.slice_in_dim(cells, cells.shape[dim] - width, cells.shape[dim], axis=dim)
        cells = jnp.concatenate(
            [
                lax.ppermute(tail, axis, [(i, (i + 1) % count) for i in range(ends)]),
                cells,
                lax.ppermute(head, axis, [((i + 1) % count, i) for i in range(ends)]),
            ],
            axis=dim,
        )
    return cells


def body(
    adj_out,
    advect,
    viscosity,
    body_mask,
    marker_x,
    marker_z,
    marker_y,
    drag_weight,
    inv_x,
    inv_y,
    inv_z,
):
    fields, x_rows, z_rows, y_cells = adj_out.shape
    x_offset = lax.axis_index("grp") * x_rows
    z_offset = lax.axis_index("slab") * z_rows
    local_x = marker_x - x_offset
    local_z = marker_z - z_offset
    inside = (local_x >= 0) & (local_x < x_rows) & (local_z >= 0) & (local_z < z_rows)
    flat_index = jnp.where(inside, (local_x * z_rows + local_z) * y_cells + marker_y, 0)
    pushed = jax.ops.segment_sum(
        jnp.where(inside, drag_weight, 0.0), flat_index, num_segments=x_rows * z_rows * y_cells
    )
    seeded = adj_out.at[0].add(pushed.reshape(x_rows, z_rows, y_cells))
    zlines = lax.all_to_all(seeded, "slab", split_axis=1, concat_axis=2, tiled=True)
    zlines = jnp.einsum("jk,cxjy->cxky", inv_z, zlines, precision=highest)
    zlines = jnp.einsum("jk,cxzj->cxzk", inv_y, zlines, precision=highest)
    returned = lax.all_to_all(zlines, "slab", split_axis=2, concat_axis=1, tiled=True)
    solved = jnp.einsum(
        "jk,cjzy->ckzy",
        inv_x,
        lax.all_gather(returned, "grp", axis=1, tiled=True),
        precision=highest,
    )
    masked = solved * body_mask.astype(jnp.float32)
    rimmed = extended(masked, (("slab", 2), ("grp", 1)), 1)
    centre = rimmed[:, 1:-1, 1:-1, :]
    y_padded = jnp.pad(centre, ((0, 0), (0, 0), (0, 0), (1, 1)))
    grad_x = (rimmed[:, 2:, 1:-1, :] - rimmed[:, :-2, 1:-1, :]) * 0.5
    grad_z = (rimmed[:, 1:-1, 2:, :] - rimmed[:, 1:-1, :-2, :]) * 0.5
    grad_y = (y_padded[..., 2:] - y_padded[..., :-2]) * 0.5
    laplace = (
        rimmed[:, 2:, 1:-1, :]
        + rimmed[:, :-2, 1:-1, :]
        + rimmed[:, 1:-1, 2:, :]
        + rimmed[:, 1:-1, :-2, :]
        + y_padded[..., 2:]
        + y_padded[..., :-2]
        - 6.0 * centre
    )
    velocity = advect.astype(jnp.float32)
    viscous = viscosity.astype(jnp.float32)
    change = velocity[0] * grad_x + velocity[1] * grad_z + velocity[2] * grad_y + viscous * laplace
    return centre + time_step * change


def solution(mesh):
    in_specs = (
        P(None, "grp", "slab", None),
        P(None, "grp", "slab", None),
        P("grp", "slab", None),
        P("grp", "slab", None),
        P(),
        P(),
        P(),
        P(),
        P(None, "grp"),
        P(),
        P(),
    )
    out_specs = P(None, "grp", "slab", None)
    return jax.shard_map(body, mesh=mesh, in_specs=in_specs, out_specs=out_specs, check_vma=False)
```

profile of v0, /device:TPU:352, one launch (start us, length us, event | category | flops | bytes accessed | tf_op | source)
XLA Modules:
  0.0 591.5 jit_solution(2021794597790402186)
XLA Ops:
  6.5 0.8 add_select_fusion
  7.3 0.7 broadcast_select_fusion
  8.1 14.8 %scatter_custom_fusion = f32[65536]{0:T(1024)S(1)} fusion(s32[2048]{0:T(1024)S(1)} %add_select_fusion, f32[2048]{0:T(1024)S(1)} %broadcast_select_fusion, f32[]{:T(128)} %constant.45.clone.1), kind=kCustom, calls=%fused_computation.27 | custom fusion | flops 2048 | bytes 262148 | tf_op jit(solution)/shard_map/scatter-add | solution.py:47
  23.0 1.5 copy.57
  24.6 68.9 %all_to_all.21 = f32[5,64,4,256]{3,2,0,1:T(4,128)S(1)} all-to-all(f32[5,64,4,256]{3,2,0,1:T(4,128)S(1)} %fusion.4), channel_id=1, replica_groups=mesh['slab'=64,'grp'=8] {'slab'}, dimensions={1} | all-to-all | bytes 2621440 | tf_op jit(solution)/shard_map/all_to_all | solution.py:51
  93.8 0.5 reshape.63
  94.3 2.2 convolution_bitcast_fusion.1
  96.5 2.3 convolution_bitcast_fusion
  98.8 1.3 copy.61
  100.1 70.3 %all_to_all.22 = f32[5,1,256,256]{3,1,0,2:T(1,128)S(1)} all-to-all(f32[5,1,256,256]{3,1,0,2:T(1,128)S(1)} %copy.61), channel_id=1, replica_groups=mesh['slab'=64,'grp'=8] {'slab'}, dimensions={2} | all-to-all | bytes 2621440 | tf_op jit(solution)/shard_map/all_to_all | solution.py:54
  170.4 0.3 copy.75
  170.7 1.8 copy.63
  172.5 0.9 copy-done.2
  173.6 324.0 %all-gather.2.cloned.1.call-done = f32[5,512,4,256]{3,1,2,0:T(8,128)} async-done(((f32[5,64,4,256]{3,1,2,0:T(8,128)}), f32[5,512,4,256]{3,1,2,0:T(8,128)}) %all-gather.2.cloned.1.call-update) | async-done | bytes 10485776 | tf_op jit(solution)/shard_map/all_gather | solution.py:58
  497.6 9.5 %fusion = f32[5,64,4,256]{3,1,2,0:T(8,128)S(1)} fusion(f32[5,512,4,256]{3,1,2,0:T(8,128)} %all-gather.2.cloned.1.call-done, f32[64,4,256]{2,0,1:T(8,128)S(1)} %copy.64, f32[512,64]{0,1:T(8,128)S(1)} %copy-done.4), kind=kOutput, calls=%fused_computation.6 | convolution fusion | flops 2013593600 | bytes 12189696 | tf_op jit(solution)/shard_map/jk,cjzy->ckzy/dot_general | solution.py:55
  507.2 2.1 collective-permute-start
  509.3 38.0 %collective-permute-start.1 = (f32[5,64,1,256]{3,1,2,0:T(8,128)S(1)}, f32[5,64,1,256]{3,1,2,0:T(8,128)S(1)}, u32[]{:S(2)}, u32[]{:S(2)}) collective-permute-start(f32[5,64,1,256]{3,1,2,0:T(8,128)S(1)} %get-tuple-element.20), channel_id=1, source_target_pairs={{8,0},{16,8},{24,16},{32,24},{40,32},{48,40},{56,48},{64,56},{72,6... | collective-permute-start | bytes 983048 | tf_op jit(solution)/shard_map/ppermute | solution.py:20
  547.5 2.7 collective-permute-done
  550.1 2.1 collective-permute-done.1
  552.3 11.7 %collective-permute-start.2 = (f32[5,1,6,256]{3,1,2,0:T(1,128)S(1)}, f32[5,1,6,256]{3,1,2,0:T(1,128)S(1)}, u32[]{:S(2)}, u32[]{:S(2)}) collective-permute-start(f32[5,1,6,256]{3,1,2,0:T(1,128)S(1)} %get-tuple-element.18), channel_id=1, source_target_pairs={{1,0},{2,1},{3,2},{4,3},{5,4},{6,5},{7,6},{9,8},{10,9},{11,10},{12... | collective-permute-start | bytes 92168 | tf_op jit(solution)/shard_map/ppermute | solution.py:20
  564.0 2.1 collective-permute-start.3
  566.5 14.3 %collective-permute-done.3 = f32[5,1,6,256]{3,1,2,0:T(1,128)S(1)} collective-permute-done((f32[5,1,6,256]{3,1,2,0:T(1,128)S(1)}, f32[5,1,6,256]{3,1,2,0:T(1,128)S(1)}, u32[]{:S(2)}, u32[]{:S(2)}) %collective-permute-start.3) | collective-permute-done | bytes 30752 | tf_op jit(solution)/shard_map/ppermute | solution.py:18
  580.7 2.0 multiply_add_fusion
  582.8 1.9 copy.69
  (27 shorter events, 1.2 us)
Async XLA Ops:
  6.5 87.7 %copy-start = (f32[256,256]{1,0:T(8,128)S(1)}, f32[256,256]{1,0:T(8,128)}, u32[]{:S(2)}) copy-start(f32[256,256]{1,0:T(8,128)} %param.23) | copy-start | bytes 786436
  6.5 491.1 %all-gather.2.cloned.1.call-start = ((), (), s32[]{:S(2)}) async-start(), calls=%async_computation.2 | async-start | bytes 11796480 | tf_op jit(solution)/shard_map/all_gather | solution.py:58
  94.2 2.2 copy-start.3
  172.5 0.9 copy-start.2
  172.5 325.1 %copy-start.4 = (f32[512,64]{0,1:T(8,128)S(1)}, f32[512,64]{0,1:T(8,128)}, u32[]{:S(2)}) copy-start(f32[512,64]{0,1:T(8,128)} %param.21) | copy-start | bytes 393220
  507.1 40.2 %copy-start.1 = (bf16[3,64,4,256]{3,2,1,0:T(4,128)(2,1)S(1)}, bf16[3,64,4,256]{3,2,1,0:T(4,128)(2,1)}, u32[]{:S(2)}) copy-start(bf16[3,64,4,256]{3,2,1,0:T(4,128)(2,1)} %param.14) | copy-start | bytes 1179652
  507.2 42.9 %collective-permute-start = (f32[5,64,1,256]{3,1,2,0:T(8,128)S(1)}, f32[5,64,1,256]{3,1,2,0:T(8,128)S(1)}, u32[]{:S(2)}, u32[]{:S(2)}) collective-permute-start(f32[5,64,1,256]{3,1,2,0:T(8,128)S(1)} %get-tuple-element.19), channel_id=1, source_target_pairs={{0,8},{8,16},{16,24},{24,32},{32,40},{40,48},{48,56},{56,64},{64,7... | collective-permute-start | bytes 983048 | tf_op jit(solution)/shard_map/ppermute | solution.py:18
  509.3 42.9 %collective-permute-start.1 = (f32[5,64,1,256]{3,1,2,0:T(8,128)S(1)}, f32[5,64,1,256]{3,1,2,0:T(8,128)S(1)}, u32[]{:S(2)}, u32[]{:S(2)}) collective-permute-start(f32[5,64,1,256]{3,1,2,0:T(8,128)S(1)} %get-tuple-element.20), channel_id=1, source_target_pairs={{8,0},{16,8},{24,16},{32,24},{40,32},{48,40},{56,48},{64,56},{72,6... | collective-permute-start | bytes 983048 | tf_op jit(solution)/shard_map/ppermute | solution.py:20
  552.3 14.2 %collective-permute-start.2 = (f32[5,1,6,256]{3,1,2,0:T(1,128)S(1)}, f32[5,1,6,256]{3,1,2,0:T(1,128)S(1)}, u32[]{:S(2)}, u32[]{:S(2)}) collective-permute-start(f32[5,1,6,256]{3,1,2,0:T(1,128)S(1)} %get-tuple-element.18), channel_id=1, source_target_pairs={{1,0},{2,1},{3,2},{4,3},{5,4},{6,5},{7,6},{9,8},{10,9},{11,10},{12... | collective-permute-start | bytes 92168 | tf_op jit(solution)/shard_map/ppermute | solution.py:20
  564.0 2.5 copy-start.5
  564.0 16.7 %collective-permute-start.3 = (f32[5,1,6,256]{3,1,2,0:T(1,128)S(1)}, f32[5,1,6,256]{3,1,2,0:T(1,128)S(1)}, u32[]{:S(2)}, u32[]{:S(2)}) collective-permute-start(f32[5,1,6,256]{3,1,2,0:T(1,128)S(1)} %get-tuple-element.17), channel_id=1, source_target_pairs={{0,1},{1,2},{2,3},{3,4},{4,5},{5,6},{6,7},{8,9},{9,10},{10,11},{11... | collective-permute-start | bytes 92168 | tf_op jit(solution)/shard_map/ppermute | solution.py:18
Sparse Core Ops, SparseCore 0:
  172.7 324.8 all-gather.1
where the time goes:
time: 592 us
  waiting for transfers between devices  343 us (58%)
  blocking collectives  139 us (23%)
  starting transfers between devices  53.8 us (9%)
  other arithmetic  18.8 us (3%)
  matrix products  14 us (2%)
  between operations  13.6 us (2%)
  local copies, waits for them, and re-layouts  8.92 us (2%)
    all_gather x1, waiting for transfers between devices, body(): lax.all_gather(returned, 'grp', axis=1, tiled=True)  324 us
    all_to_all x1, blocking collectives, body(): lax.all_to_all(zlines, 'slab', split_axis=2, concat_axis=1, tiled=True)  70.3 us
    all_to_all x1, blocking collectives, body(): lax.all_to_all(seeded, 'slab', split_axis=1, concat_axis=2, tiled=True)  68.9 us
    ppermute x2, starting transfers between devices, extended(): lax.ppermute(head, axis, [((i + 1) % count, i) for i in range(ends)])  49.7 us
    ppermute x2, waiting for transfers between devices, extended(): lax.ppermute(tail, axis, [(i, (i + 1) % count) for i in range(ends)])  17 us
    scatter-add x1, other arithmetic, body(): jax.ops.segment_sum(jnp.where(inside, drag_weight, 0.0), flat_index, num_...  14.8 us
  transfers between devices with their start and end apart: 5, of which 4 were waited for; matrix products, arithmetic and copies ran while one was open for 0% of the time, Pallas kernels for 0%

commit v1 on v0

--- a/solution.py
+++ b/solution.py
@@ -48,7 +48,10 @@
         jnp.where(inside, drag_weight, 0.0), flat_index, num_segments=x_rows * z_rows * y_cells
     )
     seeded = adj_out.at[0].add(pushed.reshape(x_rows, z_rows, y_cells))
-    zlines = lax.all_to_all(seeded, "slab", split_axis=1, concat_axis=2, tiled=True)
+    size = lax.axis_size("slab")
+    blocks = jnp.stack(jnp.split(seeded, size, axis=1), axis=0)
+    blocks = lax.all_to_all(blocks, "slab", split_axis=0, concat_axis=0)
+    zlines = jnp.concatenate(blocks, axis=2)
     zlines = jnp.einsum("jk,cxjy->cxky", inv_z, zlines, precision=highest)
     zlines = jnp.einsum("jk,cxzj->cxzk", inv_y, zlines, precision=highest)
     returned = lax.all_to_all(zlines, "slab", split_axis=2, concat_axis=1, tiled=True)

time: 592 us -> 591 us (level)
  no operation moved by 1% of the time
where the time goes in v1:
time: 591 us; the launch traced here: 590 us
  waiting for transfers between devices  343 us (58%)
  blocking collectives  139 us (24%)
  starting transfers between devices  53.9 us (9%)
  other arithmetic  17.3 us (3%)
  matrix products  14 us (2%)
  between operations  14 us (2%)
  local copies, waits for them, and re-layouts  8.87 us (2%)
    all_gather x1, waiting for transfers between devices, body(): lax.all_gather(returned, 'grp', axis=1, tiled=True)  324 us
    all_to_all x1, blocking collectives, body(): lax.all_to_all(zlines, 'slab', split_axis=2, concat_axis=1, tiled=True)  70.3 us
    all_to_all x1, blocking collectives, body(): blocks = lax.all_to_all(blocks, 'slab', split_axis=0, concat_axis=0)  68.9 us
    ppermute x2, starting transfers between devices, extended(): lax.ppermute(head, axis, [((i + 1) % count, i) for i in range(ends)])  49.7 us
    ppermute x2, waiting for transfers between devices, extended(): lax.ppermute(tail, axis, [(i, (i + 1) % count) for i in range(ends)])  17 us
    scatter-add x1, other arithmetic, body(): jax.ops.segment_sum(jnp.where(inside, drag_weight, 0.0), flat_index, num_...  14.8 us
  transfers between devices with their start and end apart: 5, of which 4 were waited for; matrix products, arithmetic and copies ran while one was open for 0% of the time, Pallas kernels for 0%

profile of v1, /device:TPU:352, one launch (start us, length us, event | category | flops | bytes accessed | tf_op | source)
XLA Modules:
  0.0 590.4 jit_solution(14619964165415629873)
XLA Ops:
  6.6 0.7 copy-done.8
  7.4 14.8 %scatter_custom_fusion = f32[65536]{0:T(1024)S(1)} fusion(s32[2048]{0:T(1024)S(1)} %add_select_fusion, f32[2048]{0:T(1024)S(1)} %broadcast_select_fusion, f32[]{:T(128)} %constant.45.clone.1), kind=kCustom, calls=%fused_computation.90 | custom fusion | flops 2048 | bytes 262148 | tf_op jit(solution)/shard_map/scatter-add | solution.py:47
  23.5 68.9 %all_to_all.17 = f32[64,5,1,4,256]{4,3,1,2,0:T(4,128)S(1)} all-to-all(f32[64,5,1,4,256]{4,3,1,2,0:T(4,128)S(1)} %constant_dynamic-update-slice_fusion), channel_id=1, replica_groups=mesh['slab'=64,'grp'=8] {'slab'}, dimensions={0} | all-to-all | bytes 2621440 | tf_op jit(solution)/shard_map/all_to_all | solution.py:53
  92.4 0.2 copy.368
  92.6 0.5 reshape.65
  93.1 2.2 convolution_bitcast_fusion.1
  95.4 2.3 convolution_bitcast_fusion
  97.6 1.3 copy.371
  99.0 70.3 %all_to_all.18 = f32[5,1,256,256]{3,1,0,2:T(1,128)S(1)} all-to-all(f32[5,1,256,256]{3,1,0,2:T(1,128)S(1)} %copy.371), channel_id=1, replica_groups=mesh['slab'=64,'grp'=8] {'slab'}, dimensions={2} | all-to-all | bytes 2621440 | tf_op jit(solution)/shard_map/all_to_all | solution.py:57
  169.3 0.3 copy.385
  169.6 1.8 copy.373
  171.4 0.9 copy-done.3
  172.4 324.0 %all-gather.2.cloned.1.call-done = f32[5,512,4,256]{3,1,2,0:T(8,128)} async-done(((f32[5,64,4,256]{3,1,2,0:T(8,128)}), f32[5,512,4,256]{3,1,2,0:T(8,128)}) %all-gather.2.cloned.1.call-update) | async-done | bytes 10485776 | tf_op jit(solution)/shard_map/all_gather | solution.py:61
  496.5 9.6 %fusion = f32[5,64,4,256]{3,1,2,0:T(8,128)S(1)} fusion(f32[5,512,4,256]{3,1,2,0:T(8,128)} %all-gather.2.cloned.1.call-done, f32[64,4,256]{2,0,1:T(8,128)S(1)} %copy.374, f32[512,64]{0,1:T(8,128)S(1)} %copy-done.5), kind=kOutput, calls=%fused_computation.6 | convolution fusion | flops 2013593600 | bytes 12189696 | tf_op jit(solution)/shard_map/jk,cjzy->ckzy/dot_general | solution.py:58
  506.1 2.1 collective-permute-start
  508.1 38.0 %collective-permute-start.1 = (f32[5,64,1,256]{3,1,2,0:T(8,128)S(1)}, f32[5,64,1,256]{3,1,2,0:T(8,128)S(1)}, u32[]{:S(2)}, u32[]{:S(2)}) collective-permute-start(f32[5,64,1,256]{3,1,2,0:T(8,128)S(1)} %get-tuple-element.20), channel_id=1, source_target_pairs={{8,0},{16,8},{24,16},{32,24},{40,32},{48,40},{56,48},{64,56},{72,6... | collective-permute-start | bytes 983048 | tf_op jit(solution)/shard_map/ppermute | solution.py:20
  546.3 2.7 collective-permute-done
  549.0 2.1 collective-permute-done.1
  551.1 11.7 %collective-permute-start.2 = (f32[5,1,6,256]{3,1,2,0:T(1,128)S(1)}, f32[5,1,6,256]{3,1,2,0:T(1,128)S(1)}, u32[]{:S(2)}, u32[]{:S(2)}) collective-permute-start(f32[5,1,6,256]{3,1,2,0:T(1,128)S(1)} %get-tuple-element.18), channel_id=1, source_target_pairs={{1,0},{2,1},{3,2},{4,3},{5,4},{6,5},{7,6},{9,8},{10,9},{11,10},{12... | collective-permute-start | bytes 92168 | tf_op jit(solution)/shard_map/ppermute | solution.py:20
  562.9 2.1 collective-permute-start.3
  564.9 0.2 fusion.3
  565.3 14.3 %collective-permute-done.3 = f32[5,1,6,256]{3,1,2,0:T(1,128)S(1)} collective-permute-done((f32[5,1,6,256]{3,1,2,0:T(1,128)S(1)}, f32[5,1,6,256]{3,1,2,0:T(1,128)S(1)}, u32[]{:S(2)}, u32[]{:S(2)}) %collective-permute-start.3) | collective-permute-done | bytes 30752 | tf_op jit(solution)/shard_map/ppermute | solution.py:18
  579.6 2.0 multiply_add_fusion
  581.6 1.9 copy.379
  (100 shorter events, 1.5 us)
Async XLA Ops:
  6.5 86.6 %copy-start = (f32[256,256]{1,0:T(8,128)S(1)}, f32[256,256]{1,0:T(8,128)}, u32[]{:S(2)}) copy-start(f32[256,256]{1,0:T(8,128)} %param.23) | copy-start | bytes 786436
  6.5 15.8 %copy-start.1 = (f32[5,64,4,256]{3,2,1,0:T(4,128)S(1)}, f32[5,64,4,256]{3,2,1,0:T(4,128)}, u32[]{:S(2)}) copy-start(f32[5,64,4,256]{3,2,1,0:T(4,128)} %param.13) | copy-start | bytes 3932164
  6.5 0.8 copy-start.8
  6.5 0.8 copy-start.7
  6.5 0.8 copy-start.9
  6.5 0.9 copy-start.10
  6.6 489.9 %all-gather.2.cloned.1.call-start = ((), (), s32[]{:S(2)}) async-start(), calls=%async_computation.2 | async-start | bytes 11796480 | tf_op jit(solution)/shard_map/all_gather | solution.py:61
  93.1 2.2 copy-start.4
  171.4 0.9 copy-start.3
  171.4 325.1 %copy-start.5 = (f32[512,64]{0,1:T(8,128)S(1)}, f32[512,64]{0,1:T(8,128)}, u32[]{:S(2)}) copy-start(f32[512,64]{0,1:T(8,128)} %param.21) | copy-start | bytes 393220
  506.0 40.2 %copy-start.2 = (bf16[3,64,4,256]{3,2,1,0:T(4,128)(2,1)S(1)}, bf16[3,64,4,256]{3,2,1,0:T(4,128)(2,1)}, u32[]{:S(2)}) copy-start(bf16[3,64,4,256]{3,2,1,0:T(4,128)(2,1)} %param.14) | copy-start | bytes 1179652
  506.1 42.9 %collective-permute-start = (f32[5,64,1,256]{3,1,2,0:T(8,128)S(1)}, f32[5,64,1,256]{3,1,2,0:T(8,128)S(1)}, u32[]{:S(2)}, u32[]{:S(2)}) collective-permute-start(f32[5,64,1,256]{3,1,2,0:T(8,128)S(1)} %get-tuple-element.19), channel_id=1, source_target_pairs={{0,8},{8,16},{16,24},{24,32},{32,40},{40,48},{48,56},{56,64},{64,7... | collective-permute-start | bytes 983048 | tf_op jit(solution)/shard_map/ppermute | solution.py:18
  508.1 42.9 %collective-permute-start.1 = (f32[5,64,1,256]{3,1,2,0:T(8,128)S(1)}, f32[5,64,1,256]{3,1,2,0:T(8,128)S(1)}, u32[]{:S(2)}, u32[]{:S(2)}) collective-permute-start(f32[5,64,1,256]{3,1,2,0:T(8,128)S(1)} %get-tuple-element.20), channel_id=1, source_target_pairs={{8,0},{16,8},{24,16},{32,24},{40,32},{48,40},{56,48},{64,56},{72,6... | collective-permute-start | bytes 983048 | tf_op jit(solution)/shard_map/ppermute | solution.py:20
  551.1 14.2 %collective-permute-start.2 = (f32[5,1,6,256]{3,1,2,0:T(1,128)S(1)}, f32[5,1,6,256]{3,1,2,0:T(1,128)S(1)}, u32[]{:S(2)}, u32[]{:S(2)}) collective-permute-start(f32[5,1,6,256]{3,1,2,0:T(1,128)S(1)} %get-tuple-element.18), channel_id=1, source_target_pairs={{1,0},{2,1},{3,2},{4,3},{5,4},{6,5},{7,6},{9,8},{10,9},{11,10},{12... | collective-permute-start | bytes 92168 | tf_op jit(solution)/shard_map/ppermute | solution.py:20
  562.9 2.5 copy-start.6
  562.9 16.7 %collective-permute-start.3 = (f32[5,1,6,256]{3,1,2,0:T(1,128)S(1)}, f32[5,1,6,256]{3,1,2,0:T(1,128)S(1)}, u32[]{:S(2)}, u32[]{:S(2)}) collective-permute-start(f32[5,1,6,256]{3,1,2,0:T(1,128)S(1)} %get-tuple-element.17), channel_id=1, source_target_pairs={{0,1},{1,2},{2,3},{3,4},{4,5},{5,6},{6,7},{8,9},{9,10},{10,11},{11... | collective-permute-start | bytes 92168 | tf_op jit(solution)/shard_map/ppermute | solution.py:18
Sparse Core Ops, SparseCore 0:
  171.5 324.8 all-gather.1
